TPU v7x, 32 devices: a whole 2x2x4 slice. The times are simulated.
32 devices in a mesh: dp: 4 (over y, x), row: 2 (over core), col: 4 (over z).
Axes of the slice: x: 2, y: 2, z: 4, core: 2. Of those that a mesh axis runs over, the one named last changes fastest.
Arguments:
- states: bfloat16 [25088, 1024], P(('dp', 'row', 'col')), may hold values from -6 to 6
- ln1_gain: bfloat16 [1024], P('row'), may hold values from 0.5 to 1.5
- ln1_bias: bfloat16 [1024], P('row'), may hold values from -0.59765625 to 0.59765625
- w_qkv: bfloat16 [1024, 3, 1024], P('row', None, 'col'), may hold values from -0.1875 to 0.1875
- q_bias: bfloat16 [1024], P('col'), may hold values from -1.796875 to 1.796875
- v_bias: bfloat16 [1024], P('col'), may hold values from -0.29882812 to 0.29882812
- w_proj: bfloat16 [1024, 1024], P('col', 'row'), may hold values from -0.75 to 0.75
- proj_bias: bfloat16 [1024], P('row'), may hold values from -0.59765625 to 0.59765625
- ln2_gain: bfloat16 [1024], P('row'), may hold values from 0.5 to 1.5
- ln2_bias: bfloat16 [1024], P('row'), may hold values from -0.59765625 to 0.59765625
- w_fc1: bfloat16 [1024, 4096], P('row', 'col'), may hold values from -0.1875 to 0.1875
- fc1_bias: bfloat16 [4096], P('col'), may hold values from -0.59765625 to 0.59765625
- w_fc2: bfloat16 [4096, 1024], P('col', 'row'), may hold values from -0.09375 to 0.09375
- fc2_bias: bfloat16 [1024], P('row'), may hold values from -0.59765625 to 0.59765625
- teacher: bfloat16 [25088, 1024], P(('dp', 'row', 'col')), may hold values from -6 to 6
- loss_mask: int32 [25088], replicated, may hold values 0 or 1
- lengths: int32 [16], replicated, may hold values from 784 to 1568, as said below
Outputs:
- states_out: bfloat16 [25088, 1024], P(('dp', 'row', 'col'))
- loss: float32 [], replicated
- grad_states: bfloat16 [25088, 1024], P(('dp', 'row', 'col'))
- grad_ln1_gain: float32 [1024], P('row')
- grad_ln1_bias: float32 [1024], P('row')
- grad_w_qkv: float32 [1024, 3, 1024], P('row', None, 'col')
- grad_q_bias: float32 [1024], P('col')
- grad_v_bias: float32 [1024], P('col')
- grad_w_proj: float32 [1024, 1024], P('col', 'row')
- grad_proj_bias: float32 [1024], P('row')
- grad_ln2_gain: float32 [1024], P('row')
- grad_ln2_bias: float32 [1024], P('row')
- grad_w_fc1: float32 [1024, 4096], P('row', 'col')
- grad_fc1_bias: float32 [4096], P('col')
- grad_w_fc2: float32 [4096, 1024], P('col', 'row')
- grad_fc2_bias: float32 [1024], P('row')
Inputs may be any that keep to these rules, and one draw needn't show every extreme that they name: `lengths`: each entry is the number of real tube tokens of one clip, from 784 to 1568; some clip has all 1568. Positions at or beyond it are padding.
All inputs are finite; a program needn't handle non-finite values.
Results may differ from a plain program's by a relative error of at most 0.012.
The roundings to bfloat16 on the way count: a program that leaves them out, or rounds other values in their place, can miss the bound.
Values may be sent and summed in bfloat16 or wider, within the bound.
No kernel may reach another device: no remote copies, remote signals or barrier semaphores. Data moves between devices by JAX's collectives and lax.ppermute only.
A program may use at most 320 MiB of HBM per device.

v0:
```python
import jax
import jax.numpy as jnp
from jax import lax
from jax.sharding import PartitionSpec as P

HD = 64
L = 1568
EPSILON = 1e-06
MASKED = -1e30
ROOT_HALF = 0.7071067811865476
DENSITY_FACTOR = 0.3989422804014327


def normalize(values, factor, offset):
    centered = values - jnp.mean(values, axis=-1, keepdims=True)
    spread = lax.rsqrt(jnp.mean(centered * centered, axis=-1, keepdims=True) + EPSILON)
    normal = centered * spread
    return (normal * factor + offset, normal, spread)


def norm_back(upstream, normal, spread, factor):
    inner = upstream * factor
    center_term = jnp.mean(inner, axis=-1, keepdims=True)
    slope_term = jnp.mean(inner * normal, axis=-1, keepdims=True)
    back = spread * (inner - center_term - normal * slope_term)
    return (back, jnp.sum(upstream * normal, axis=0), jnp.sum(upstream, axis=0))


def gelu_value(values):
    return values * (0.5 * (1.0 + lax.erf(values * ROOT_HALF)))


def gelu_slope(values):
    normal_cdf = 0.5 * (1.0 + lax.erf(values * ROOT_HALF))
    return normal_cdf + values * jnp.exp(-0.5 * values * values) * DENSITY_FACTOR


def masked_scores(queries, key_rows, length, score_scale):
    logits = (
        jnp.einsum("ihd,jhd->hij", queries, key_rows, preferred_element_type=jnp.float32)
        * score_scale
    )
    keep = jnp.arange(key_rows.shape[0]) < length
    return jnp.where(keep[None, None, :], logits, MASKED)


def attend_clip(packed, length, score_scale):
    half_span = packed.shape[0] // 2
    key_rows = packed[:, 1]
    value_rows = packed[:, 2]
    pieces = []
    totals = []
    for block_index in range(2):
        queries = packed[block_index * half_span : (block_index + 1) * half_span, 0]
        logits = masked_scores(queries, key_rows, length, score_scale)
        peak = jnp.max(logits, axis=-1, keepdims=True)
        total = peak + jnp.log(jnp.sum(jnp.exp(logits - peak), axis=-1, keepdims=True))
        weights = jnp.exp(logits - total).astype(jnp.bfloat16)
        pieces.append(
            jnp.einsum("hij,jhd->ihd", weights, value_rows, preferred_element_type=jnp.float32)
        )
        totals.append(total[..., 0])
    return (jnp.concatenate(pieces, 0), jnp.concatenate(totals, 1))


def attend_clip_back(packed, length, totals, upstream, score_scale):
    half_span = packed.shape[0] // 2
    key_rows = packed[:, 1]
    value_rows = packed[:, 2]
    grad_keys = jnp.zeros(key_rows.shape, jnp.float32)
    grad_values = jnp.zeros(value_rows.shape, jnp.float32)
    grad_queries = []
    for block_index in range(2):
        first = block_index * half_span
        queries = packed[first : first + half_span, 0]
        logits = masked_scores(queries, key_rows, length, score_scale)
        probs = jnp.exp(logits - totals[:, first : first + half_span][..., None])
        incoming = upstream[first : first + half_span]
        grad_values = grad_values + jnp.einsum(
            "hij,ihd->jhd", probs.astype(jnp.bfloat16), incoming, preferred_element_type=jnp.float32
        )
        grad_probs = jnp.einsum(
            "ihd,jhd->hij", incoming, value_rows, preferred_element_type=jnp.float32
        )
        grad_logits = (
            probs * (grad_probs - jnp.sum(probs * grad_probs, axis=-1, keepdims=True))
        ).astype(jnp.bfloat16)
        grad_queries.append(
            jnp.einsum("hij,jhd->ihd", grad_logits, key_rows, preferred_element_type=jnp.float32)
            * score_scale
        )
        grad_keys = (
            grad_keys
            + jnp.einsum("hij,ihd->jhd", grad_logits, queries, preferred_element_type=jnp.float32)
            * score_scale
        )
    return jnp.stack([jnp.concatenate(grad_queries, 0), grad_keys, grad_values], axis=1)


def local(
    states,
    ln1_gain,
    ln1_bias,
    w_qkv,
    q_bias,
    v_bias,
    w_proj,
    proj_bias,
    ln2_gain,
    ln2_bias,
    w_fc1,
    fc1_bias,
    w_fc2,
    fc2_bias,
    teacher,
    loss_mask,
    lengths,
):
    row_count = lax.axis_size("row")
    col_count = lax.axis_size("col")
    col_index = lax.axis_index("col")
    group_index = lax.axis_index("dp") * row_count + lax.axis_index("row")
    local_rows = states.shape[0]
    width = states.shape[1]
    group_rows = local_rows * col_count
    clip_count = group_rows // L
    head_width = w_qkv.shape[2]
    heads_here = head_width // HD
    hidden_width = w_fc1.shape[1]
    score_scale = HD ** (-0.5)
    vectors = jnp.stack([ln1_gain, ln1_bias, proj_bias, ln2_gain, ln2_bias, fc2_bias])
    qkv_full, proj_full, fc1_full, fc2_full, vector_full = (
        lax.all_gather(w_qkv, "row", axis=0, tiled=True),
        lax.all_gather(w_proj, "row", axis=1, tiled=True),
        lax.all_gather(w_fc1, "row", axis=0, tiled=True),
        lax.all_gather(w_fc2, "row", axis=1, tiled=True),
        lax.all_gather(vectors, "row", axis=1, tiled=True),
    )
    vector_full = vector_full.astype(jnp.float32)
    gain_one = vector_full[0]
    shift_one = vector_full[1]
    bias_proj = vector_full[2]
    gain_two = vector_full[3]
    shift_two = vector_full[4]
    bias_two = vector_full[5]
    all_clips = lengths.shape[0]
    valid_all = (
        loss_mask.reshape(all_clips, L) * (jnp.arange(L)[None, :] < lengths[:, None])
    ).astype(jnp.float32)
    valid_total = jnp.maximum(jnp.sum(valid_all), 1.0)
    first_row = (group_index * col_count + col_index) * local_rows
    valid = lax.dynamic_slice_in_dim(valid_all.reshape(all_clips * L), first_row, local_rows)
    my_lengths = lax.dynamic_slice_in_dim(lengths, group_index * clip_count, clip_count)
    inputs = states.astype(jnp.float32)
    norm_one, unit_one, spread_one = normalize(inputs, gain_one, shift_one)
    norm_one = norm_one.astype(jnp.bfloat16)
    tokens_one = lax.all_gather(norm_one, "col", axis=0, tiled=True)
    qkv_matrix = qkv_full.reshape(width, 3 * head_width)
    projected = jnp.dot(tokens_one, qkv_matrix, preferred_element_type=jnp.float32).reshape(
        group_rows, 3, head_width
    )
    bias_rows = jnp.stack(
        [
            q_bias.astype(jnp.float32),
            jnp.zeros((head_width,), jnp.float32),
            v_bias.astype(jnp.float32),
        ]
    )
    packed = (projected + bias_rows[None]).astype(jnp.bfloat16)
    clips_packed = packed.reshape(clip_count, L, 3, heads_here, HD)
    attended, totals = lax.map(
        lambda element: attend_clip(element[0], element[1], score_scale), (clips_packed, my_lengths)
    )
    attended = attended.reshape(group_rows, head_width).astype(jnp.bfloat16)
    proj_whole, qkv_whole = (
        lax.all_gather(proj_full, "col", axis=0, tiled=True),
        lax.all_gather(qkv_full, "col", axis=2, tiled=True),
    )
    attended_rows = lax.all_to_all(attended, "col", split_axis=0, concat_axis=1, tiled=True)
    middle = inputs + (
        jnp.dot(attended_rows, proj_whole, preferred_element_type=jnp.float32) + bias_proj
    )
    norm_two, unit_two, spread_two = normalize(middle, gain_two, shift_two)
    norm_two = norm_two.astype(jnp.bfloat16)
    fc1_whole, fc2_whole, fc1_bias_whole = (
        lax.all_gather(fc1_full, "col", axis=1, tiled=True),
        lax.all_gather(fc2_full, "col", axis=0, tiled=True),
        lax.all_gather(fc1_bias, "col", axis=0, tiled=True),
    )
    hidden_pre = jnp.dot(
        norm_two, fc1_whole, preferred_element_type=jnp.float32
    ) + fc1_bias_whole.astype(jnp.float32)
    hidden = gelu_value(hidden_pre).astype(jnp.bfloat16)
    outputs = middle + (jnp.dot(hidden, fc2_whole, preferred_element_type=jnp.float32) + bias_two)
    differ = outputs - teacher.astype(jnp.float32)
    numerator = jnp.sum(valid[:, None] * differ * differ)
    loss_scale = all_clips * L * width / 2.0
    grad_out = loss_scale * 2.0 / (valid_total * width) * valid[:, None] * differ
    grad_low = grad_out.astype(jnp.bfloat16)
    grad_hidden = jnp.dot(grad_low, fc2_whole.T, preferred_element_type=jnp.float32)
    grad_pre = (grad_hidden * gelu_slope(hidden_pre)).astype(jnp.bfloat16)
    wide_fc2 = jnp.dot(hidden.T, grad_low, preferred_element_type=jnp.float32)
    wide_fc1 = jnp.dot(norm_two.T, grad_pre, preferred_element_type=jnp.float32)
    fc1_grad_part, fc2_grad_part = (
        lax.psum_scatter(
            wide_fc1.astype(jnp.bfloat16), "col", scatter_dimension=1, tiled=True
        ).astype(jnp.float32),
        lax.psum_scatter(
            wide_fc2.astype(jnp.bfloat16), "col", scatter_dimension=0, tiled=True
        ).astype(jnp.float32),
    )
    fc1_bias_sum = jnp.sum(grad_pre, axis=0, dtype=jnp.float32)
    grad_norm_two = jnp.dot(grad_pre, fc1_whole.T, preferred_element_type=jnp.float32)
    back_two, gain_two_grad, shift_two_grad = norm_back(
        grad_norm_two, unit_two, spread_two, gain_two
    )
    grad_mid = grad_out + back_two
    mid_low = grad_mid.astype(jnp.bfloat16)
    wide_proj = jnp.dot(attended_rows.T, mid_low, preferred_element_type=jnp.float32)
    proj_grad_part = lax.psum_scatter(
        wide_proj.astype(jnp.bfloat16), "col", scatter_dimension=0, tiled=True
    )
    grad_attended_rows = jnp.dot(mid_low, proj_whole.T, preferred_element_type=jnp.float32).astype(
        jnp.bfloat16
    )
    grad_attended = lax.all_to_all(
        grad_attended_rows, "col", split_axis=1, concat_axis=0, tiled=True
    )
    grads_packed = lax.map(
        lambda element: attend_clip_back(
            element[0], element[1], element[2], element[3], score_scale
        ),
        (clips_packed, my_lengths, totals, grad_attended.reshape(clip_count, L, heads_here, HD)),
    )
    grads_packed = grads_packed.reshape(group_rows, 3 * head_width).astype(jnp.bfloat16)
    qkv_grad_part = jnp.dot(tokens_one.T, grads_packed, preferred_element_type=jnp.float32).reshape(
        width, 3, head_width
    )
    bias_sums = jnp.sum(grads_packed.reshape(group_rows, 3, head_width), axis=0, dtype=jnp.float32)
    grads_rows = lax.all_to_all(
        grads_packed.reshape(group_rows, 3, head_width),
        "col",
        split_axis=0,
        concat_axis=2,
        tiled=True,
    )
    grad_norm_one = jnp.dot(
        grads_rows.reshape(local_rows, 3 * width),
        qkv_whole.reshape(width, 3 * width).T,
        preferred_element_type=jnp.float32,
    )
    back_one, gain_one_grad, shift_one_grad = norm_back(
        grad_norm_one, unit_one, spread_one, gain_one
    )
    grad_states = (grad_mid + back_one).astype(jnp.bfloat16)
    proj_bias_grad = jnp.sum(mid_low, axis=0, dtype=jnp.float32)
    fc2_bias_grad = jnp.sum(grad_low, axis=0, dtype=jnp.float32)
    token_vectors = jnp.stack(
        [
            gain_one_grad,
            shift_one_grad,
            proj_bias_grad,
            gain_two_grad,
            shift_two_grad,
            fc2_bias_grad,
        ]
    )
    head_vectors = lax.dynamic_update_slice(
        jnp.zeros((2, width), jnp.float32),
        jnp.stack([bias_sums[0], bias_sums[2]]),
        (0, col_index * head_width),
    )
    token_sums, head_sums, fc1_sums, loss_sum = lax.psum(
        (token_vectors, head_vectors, fc1_bias_sum, numerator), ("dp", "row", "col")
    )
    qkv_rows, proj_cols, fc1_rows, fc2_cols = (
        lax.psum_scatter(
            qkv_grad_part.astype(jnp.bfloat16), "row", scatter_dimension=0, tiled=True
        ).astype(jnp.float32),
        lax.psum_scatter(proj_grad_part, "row", scatter_dimension=1, tiled=True).astype(
            jnp.float32
        ),
        lax.psum_scatter(
            fc1_grad_part.astype(jnp.bfloat16), "row", scatter_dimension=0, tiled=True
        ).astype(jnp.float32),
        lax.psum_scatter(
            fc2_grad_part.astype(jnp.bfloat16), "row", scatter_dimension=1, tiled=True
        ).astype(jnp.float32),
    )
    qkv_grad, proj_grad, fc1_grad, fc2_grad = (
        lax.psum(qkv_rows.astype(jnp.bfloat16), "dp").astype(jnp.float32),
        lax.psum(proj_cols.astype(jnp.bfloat16), "dp").astype(jnp.float32),
        lax.psum(fc1_rows.astype(jnp.bfloat16), "dp").astype(jnp.float32),
        lax.psum(fc2_cols.astype(jnp.bfloat16), "dp").astype(jnp.float32),
    )
    half_width = width // row_count
    token_part = lax.dynamic_slice_in_dim(
        token_sums, lax.axis_index("row") * half_width, half_width, 1
    )
    head_part = lax.dynamic_slice_in_dim(head_sums, col_index * head_width, head_width, 1)
    fc1_part = lax.dynamic_slice_in_dim(fc1_sums, col_index * hidden_width, hidden_width, 0)
    loss_value = loss_sum / (valid_total * width)
    return (
        outputs.astype(jnp.bfloat16),
        loss_value,
        grad_states,
        token_part[0],
        token_part[1],
        qkv_grad,
        head_part[0],
        head_part[1],
        proj_grad,
        token_part[2],
        token_part[3],
        token_part[4],
        fc1_grad,
        fc1_part,
        fc2_grad,
        token_part[5],
    )


def solution(mesh):
    in_specs = (
        P(("dp", "row", "col"), None),
        P("row"),
        P("row"),
        P("row", None, "col"),
        P("col"),
        P("col"),
        P("col", "row"),
        P("row"),
        P("row"),
        P("row"),
        P("row", "col"),
        P("col"),
        P("col", "row"),
        P("row"),
        P(("dp", "row", "col"), None),
        P(),
        P(),
    )
    out_specs = (
        P(("dp", "row", "col"), None),
        P(),
        P(("dp", "row", "col"), None),
        P("row"),
        P("row"),
        P("row", None, "col"),
        P("col"),
        P("col"),
        P("col", "row"),
        P("row"),
        P("row"),
        P("row"),
        P("row", "col"),
        P("col"),
        P("col", "row"),
        P("row"),
    )
    return jax.shard_map(local, mesh=mesh, in_specs=in_specs, out_specs=out_specs, check_vma=False)
```

profile of v0, /device:TPU:0, one launch (start us, length us, event | category | flops | bytes accessed | tf_op | source)
XLA Modules:
  0.0 1376.4 jit_solution(3440307325007686870)
XLA Ops:
  49.4 120.7 %all-gather.9.cloned.1.call-done = bf16[3136,1024]{1,0:T(8,128)(2,1)} async-done(((bf16[784,1024]{1,0:T(8,128)(2,1)}), bf16[3136,1024]{1,0:T(8,128)(2,1)}) %all-gather.9.cloned.1.call-update) | async-done | bytes 6422544 | tf_op jit(solution)/shard_map/all_gather | solution.py:157
  179.4 14.6 %reshape.167 = bf16[2,1568,3,4,64]{4,3,1,0,2:T(4,128)(2,1)} reshape(bf16[3136,3,256]{2,0,1:T(8,128)(2,1)} %add_convert_fusion) | data formatting | bytes 9633792 | tf_op jit(solution)/shard_map/reshape | solution.py:170
  194.0 15.6 %copy.62 = bf16[2,1568,3,4,64]{1,4,3,2,0:T(8,128)(2,1)} copy(bf16[2,1568,3,4,64]{4,3,1,0,2:T(4,128)(2,1)} %reshape.167) | data formatting | bytes 9633792 | tf_op jit(solution)/shard_map/while | solution.py:171
  209.5 100.1 %while.22 = (s32[]{:T(128)}, bf16[2,1568,4,64]{1,3,2,0:T(8,128)(2,1)S(1)}, f32[2,4,1568]{2,1,0:T(4,128)S(1)}, bf16[2,1568,3,4,64]{1,4,3,2,0:T(8,128)(2,1)}, s32[2]{0:T(128)S(1)}, /*index=5*/s32[]{:T(128)}) while((s32[]{:T(128)}, bf16[2,1568,4,64]{1,3,2,0:T(8,128)(2,1)S(1)}, f32[2,4,1568]{2,1,0:T(4,128)S(1)}, ...), condition=%wide.region_7.8_spmd, body=%wide.region_2.7_spmd.sunk | while | flops 2588079616 | bytes 208644768 | solution.py:171
  324.3 78.0 %all_gather.40 = bf16[4096]{0:T(1024)(128)(2,1)S(1)} all-gather(bf16[1024]{0:T(1024)(128)(2,1)S(1)} %copy-done.38), channel_id=1, replica_groups=mesh['dp'=4,'row'=2,'col'=4] {'col'}, dimensions={0}, use_global_device_ids=true | all-gather | bytes 10240 | tf_op jit(solution)/shard_map/all_gather | solution.py:188
  412.1 15.9 %multiply_convert_fusion.2 = (bf16[784,4096]{1,0:T(8,128)(2,1)}, f32[784,4096]{1,0:T(8,128)}) fusion(f32[4096]{0:T(1024)S(1)} %convert_element_type.142, bf16[1024,4096]{1,0:T(8,128)(2,1)} %all-gather.17.cloned.1.call-done, f32[784,1024]{1,0:T(8,128)} %copy-done.10, f32[1024]{0:T(1024)S(1)} %bitcast.272, f32[1024]{0:T(1024)S(1)} %bitcast.262, ...), kind=kOutput, calls=%fused_computation.70 | convolution fusion | flops 6599950336 | bytes 30898304 | tf_op jit(solution)/shard_map/dot_general | solution.py:190
  428.0 121.4 %all-gather.21.cloned.1.call-done = bf16[4096,1024]{1,0:T(8,128)(2,1)} async-done(((bf16[1024,1024]{1,0:T(8,128)(2,1)}), bf16[4096,1024]{1,0:T(8,128)(2,1)}) %all-gather.21.cloned.1.call-update) | async-done | bytes 8388624 | tf_op jit(solution)/shard_map/all_gather | solution.py:187
  561.7 17.8 %convert_reduce_fusion = (f32[4096]{0:T(1024)}, bf16[784,4096]{1,0:T(8,128)(2,1)}) fusion(f32[784,4096]{1,0:T(8,128)} %get-tuple-element.202, f32[4096]{0:T(1024)S(1)} %convert_element_type.142, bf16[784,1024]{1,0:T(8,128)(2,1)S(1)} %get-tuple-element.162, bf16[4096,1024]{1,0:T(8,128)(2,1)} %all-gather.21.cloned.1.call-done), kind=kOutput, calls=%fused_computation.69 | convolution fusion | flops 6618411008 | bytes 29294592 | tf_op jit(solution)/shard_map/dot_general | solution.py:200
  598.9 15.1 %convolution_convert_fusion = bf16[1024,4096]{1,0:T(8,128)(2,1)} fusion(bf16[784,4096]{1,0:T(8,128)(2,1)} %get-tuple-element.207, f32[784,1024]{1,0:T(8,128)} %copy-done.10, f32[1024]{0:T(1024)S(1)} %bitcast.273, f32[1024]{0:T(1024)S(1)} %bitcast.265, f32[784]{0:T(1024)S(1)} %add_rsqrt_fusion, f32[784]{0:T(1024)S(1)} %broadcast_multiply_fusion.5), kind=kOutput, calls=%fused_computation.74 | convolution fusion | flops 6584877056 | bytes 18036864 | tf_op jit(solution)/shard_map/dot_general | solution.py:203
  622.4 14.2 %convolution_convert_fusion.1 = bf16[4096,1024]{1,0:T(8,128)(2,1)} fusion(bf16[784,4096]{1,0:T(8,128)(2,1)} %get-tuple-element.201, bf16[784,1024]{1,0:T(8,128)(2,1)S(1)} %copy-done.52), kind=kOutput, calls=%fused_computation.75 | convolution fusion | flops 6580862976 | bytes 16416768 | tf_op jit(solution)/shard_map/dot_general | solution.py:202
  636.7 61.9 %all-to-all-done.1 = bf16[784,4,256]{2,0,1:T(8,128)(2,1)S(1)} async-done(((bf16[784,4,256]{2,0,1:T(8,128)(2,1)}), bf16[784,4,256]{2,0,1:T(8,128)(2,1)S(1)}, u32[]{:S(2)}, u32[]{:S(2)}) %all-to-all-start.1) | async-done | bytes 1605664 | tf_op jit(solution)/shard_map/all_to_all | solution.py:226
  708.9 258.5 %while.23 = (s32[]{:T(128)}, bf16[2,1568,3,4,64]{1,4,3,2,0:T(8,128)(2,1)}, bf16[2,1568,3,4,64]{1,4,3,2,0:T(8,128)(2,1)}, s32[2]{0:T(128)S(1)}, f32[2,4,1568]{2,1...) while((s32[]{:T(128)}, bf16[2,1568,3,4,64]{1,4,3,2,0:T(8,128)(2,1)}, ...), condition=%wide.region_18.19_spmd, body=%wide.region_15.18_spmd.sunk | while | flops 6394224128 | bytes 484584864 | solution.py:229
  740.5 14.7 %multiply_reduce_fusion.9 = (f32[4,784]{1,0:T(4,128)S(1)}, f32[4,784,1568]{2,1,0:T(8,128)}) fusion(f32[4,784,1568]{2,1,0:T(8,128)} %fusion.126, f32[4,784]{1,0:T(4,128)S(1)} %get-tuple-element.296, bf16[1568,3,4,64]{0,3,2,1:T(8,128)(2,1)S(1)} %dynamic-slice_bitcast_fusion.21, pred[1568]{0:T(1024)(128)(4,1)S(1)} %iota_compare_fusion.6), kind=kOutput, calls=%fused_computation.25.clone.1 | convolution fusion | flops 653990848 | bytes 40677632 | tf_op jit(solution)/shard_map/while/body/eval_jaxpr/ihd,jhd->hij/dot_general | solution.py:40
  755.2 13.8 %multiply_convert_fusion.8 = bf16[4,784,1568]{2,1,0:T(8,128)(2,1)S(1)} fusion(f32[4,784,1568]{2,1,0:T(8,128)} %get-tuple-element.297, f32[4,784,1568]{2,1,0:T(8,128)} %fusion.126, f32[4,784]{1,0:T(4,128)S(1)} %get-tuple-element.301), kind=kLoop, calls=%fused_computation.24.clone.1 | loop fusion | flops 14751744 | bytes 49185024 | tf_op jit(solution)/shard_map/while/body/eval_jaxpr/convert_element_type | solution.py:87
  783.9 14.1 %multiply_reduce_fusion.10 = (f32[4,784]{1,0:T(4,128)S(1)}, f32[4,784,1568]{2,1,0:T(8,128)}) fusion(f32[4,784,1568]{2,1,0:T(8,128)} %fusion.129, f32[4,784]{1,0:T(4,128)S(1)} %get-tuple-element.298, bf16[1568,3,4,64]{0,3,2,1:T(8,128)(2,1)S(1)} %dynamic-slice_bitcast_fusion.21, pred[1568]{0:T(1024)(128)(4,1)S(1)} %iota_compare_fusion.6), kind=kOutput, calls=%fused_computation.28.clone.1 | convolution fusion | flops 653990848 | bytes 40677632 | tf_op jit(solution)/shard_map/while/body/eval_jaxpr/ihd,jhd->hij/dot_general | solution.py:40
  798.0 13.9 %multiply_convert_fusion.7 = bf16[4,784,1568]{2,1,0:T(8,128)(2,1)S(1)} fusion(f32[4,784,1568]{2,1,0:T(8,128)} %get-tuple-element.299, f32[4,784,1568]{2,1,0:T(8,128)} %fusion.129, f32[4,784]{1,0:T(4,128)S(1)} %get-tuple-element.300), kind=kLoop, calls=%fused_computation.27.clone.1 | loop fusion | flops 14751744 | bytes 49185024 | tf_op jit(solution)/shard_map/while/body/eval_jaxpr/convert_element_type | solution.py:87
  861.6 14.5 %multiply_reduce_fusion.9 = (f32[4,784]{1,0:T(4,128)S(1)}, f32[4,784,1568]{2,1,0:T(8,128)}) fusion(f32[4,784,1568]{2,1,0:T(8,128)} %fusion.126, f32[4,784]{1,0:T(4,128)S(1)} %get-tuple-element.296, bf16[1568,3,4,64]{0,3,2,1:T(8,128)(2,1)S(1)} %dynamic-slice_bitcast_fusion.21, pred[1568]{0:T(1024)(128)(4,1)S(1)} %iota_compare_fusion.6), kind=kOutput, calls=%fused_computation.25.clone.1 | convolution fusion | flops 653990848 | bytes 40677632 | tf_op jit(solution)/shard_map/while/body/eval_jaxpr/ihd,jhd->hij/dot_general | solution.py:40
  876.1 14.5 %multiply_convert_fusion.8 = bf16[4,784,1568]{2,1,0:T(8,128)(2,1)S(1)} fusion(f32[4,784,1568]{2,1,0:T(8,128)} %get-tuple-element.297, f32[4,784,1568]{2,1,0:T(8,128)} %fusion.126, f32[4,784]{1,0:T(4,128)S(1)} %get-tuple-element.301), kind=kLoop, calls=%fused_computation.24.clone.1 | loop fusion | flops 14751744 | bytes 49185024 | tf_op jit(solution)/shard_map/while/body/eval_jaxpr/convert_element_type | solution.py:87
  905.5 13.9 %multiply_reduce_fusion.10 = (f32[4,784]{1,0:T(4,128)S(1)}, f32[4,784,1568]{2,1,0:T(8,128)}) fusion(f32[4,784,1568]{2,1,0:T(8,128)} %fusion.129, f32[4,784]{1,0:T(4,128)S(1)} %get-tuple-element.298, bf16[1568,3,4,64]{0,3,2,1:T(8,128)(2,1)S(1)} %dynamic-slice_bitcast_fusion.21, pred[1568]{0:T(1024)(128)(4,1)S(1)} %iota_compare_fusion.6), kind=kOutput, calls=%fused_computation.28.clone.1 | convolution fusion | flops 653990848 | bytes 40677632 | tf_op jit(solution)/shard_map/while/body/eval_jaxpr/ihd,jhd->hij/dot_general | solution.py:40
  919.5 13.9 %multiply_convert_fusion.7 = bf16[4,784,1568]{2,1,0:T(8,128)(2,1)S(1)} fusion(f32[4,784,1568]{2,1,0:T(8,128)} %get-tuple-element.299, f32[4,784,1568]{2,1,0:T(8,128)} %fusion.129, f32[4,784]{1,0:T(4,128)S(1)} %get-tuple-element.300), kind=kLoop, calls=%fused_computation.27.clone.1 | loop fusion | flops 14751744 | bytes 49185024 | tf_op jit(solution)/shard_map/while/body/eval_jaxpr/convert_element_type | solution.py:87
  1000.4 16.0 %copy.80 = bf16[2,1568,3,4,64]{4,3,2,1,0:T(4,128)(2,1)} copy(bf16[2,1568,3,4,64]{1,4,3,2,0:T(8,128)(2,1)} %get-tuple-element.78) | data formatting | bytes 9633792 | tf_op jit(solution)/shard_map/convert_element_type | solution.py:235
  1016.4 20.6 %reshape.166 = bf16[3136,3,256]{2,1,0:T(4,128)(2,1)} reshape(bf16[2,1568,3,4,64]{4,3,2,1,0:T(4,128)(2,1)} %copy.80) | data formatting | bytes 9633792 | tf_op jit(solution)/shard_map/convert_element_type | solution.py:235
  1046.6 234.9 %all-to-all-done.2 = bf16[3136,3,256]{2,1,0:T(4,128)(2,1)} async-done(((bf16[3136,3,256]{2,1,0:T(4,128)(2,1)}), bf16[3136,3,256]{2,1,0:T(4,128)(2,1)}, u32[]{:S(2)}, u32[]{:S(2)}) %all-to-all-start.2) | async-done | bytes 4816928 | tf_op jit(solution)/shard_map/all_to_all | solution.py:240
  1310.0 39.1 %all-reduce = (f32[]{:T(128)}, f32[6,1024]{1,0:T(8,128)S(1)}, f32[2,1024]{1,0:T(2,128)S(1)}, f32[4096]{0:T(1024)S(1)}) all-reduce(f32[]{:T(128)} %get-tuple-element.181, f32[6,1024]{1,0:T(8,128)S(1)} %stack.90, f32[2,1024]{1,0:T(2,128)S(1)} %maximum_dynamic-update-slice_fusion, ...), channel_id=1, replica_groups=mesh['dp'=4,'row'=2,'col'=4] {'dp','row','col'}, use_global_device_ids=true, to_apply=%region_11.12 | all-reduce | flops 12289 | bytes 98312 | tf_op jit(solution)/shard_map/psum | solution.py:273
  (319 shorter events, 442.6 us)
Async XLA Ops:
  7.3 15.7 %all-gather.15.cloned.1.call-start = ((), (), s32[]{:S(2)}) async-start(), calls=%async_computation.13 | async-start | bytes 3145728 | tf_op jit(solution)/shard_map/all_gather | solution.py:135
  8.0 28.3 %all-gather.19.cloned.1.call-start = ((), (), s32[]{:S(2)}) async-start(), calls=%async_computation.15 | async-start | bytes 3145728 | tf_op jit(solution)/shard_map/all_gather | solution.py:136
  8.7 40.7 %all-gather.11.cloned.1.call-start = ((), (), s32[]{:S(2)}) async-start(), calls=%async_computation.11 | async-start | bytes 2359296 | tf_op jit(solution)/shard_map/all_gather | solution.py:133
  11.1 159.0 %all-gather.9.cloned.1.call-start = ((), (), s32[]{:S(2)}) async-start(), calls=%async_computation.10 | async-start | bytes 8028160 | tf_op jit(solution)/shard_map/all_gather | solution.py:157
  17.2 388.1 %all-gather.13.cloned.1.call-start = ((), (), s32[]{:S(2)}) async-start(), calls=%async_computation.12 | async-start | bytes 2621440 | tf_op jit(solution)/shard_map/all_gather | solution.py:176
  19.6 392.4 %all-gather.17.cloned.1.call-start = ((), (), s32[]{:S(2)}) async-start(), calls=%async_computation.14 | async-start | bytes 10485760 | tf_op jit(solution)/shard_map/all_gather | solution.py:186
  23.0 526.3 %all-gather.21.cloned.1.call-start = ((), (), s32[]{:S(2)}) async-start(), calls=%async_computation.16 | async-start | bytes 10485760 | tf_op jit(solution)/shard_map/all_gather | solution.py:187
  317.5 84.8 %copy-start.46 = (s32[16]{0:T(128)S(1)}, s32[16]{0:T(128)}, u32[]{:S(2)}) copy-start(s32[16]{0:T(128)} %param.37) | copy-start | bytes 196
  317.5 85.0 %copy-start.22 = (s32[25088]{0:T(1024)S(1)}, s32[25088]{0:T(1024)}, u32[]{:S(2)}) copy-start(s32[25088]{0:T(1024)} %param.36) | copy-start | bytes 301060
  320.5 84.8 %copy-start.37 = (f32[1,1024]{1,0:T(1,128)S(1)}, f32[1,1024]{1,0:T(1,128)}, u32[]{:S(2)}) copy-start(f32[1,1024]{1,0:T(1,128)} %get-tuple-element.192) | copy-start | bytes 12292
  320.5 83.4 %all-to-all-start = ((bf16[4,784,256]{2,1,0:T(8,128)(2,1)}), bf16[4,784,256]{2,1,0:T(8,128)(2,1)S(1)}, u32[]{:S(2)}, u32[]{:S(2)}) async-start(bf16[4,784,256]{2,1,0:T(8,128)(2,1)} %reshape.164), calls=%async_computation | async-start | bytes 3211264 | tf_op jit(solution)/shard_map/all_to_all | solution.py:179
  324.2 664.1 %reduce-scatter.10.cloned.1.call-start = ((), (), s32[]{:S(2)}) async-start(), calls=%async_computation.19 | async-start | bytes 2621440 | tf_op jit(solution)/shard_map/reduce_scatter | solution.py:220
  412.1 137.2 %copy-start.11 = (f32[784,1024]{1,0:T(8,128)S(1)}, f32[784,1024]{1,0:T(8,128)}, u32[]{:S(2)}) copy-start(f32[784,1024]{1,0:T(8,128)} %copy-done.10) | copy-start | bytes 9633796
  412.1 137.2 %copy-start.36 = (f32[1,1024]{1,0:T(1,128)S(1)}, f32[1,1024]{1,0:T(1,128)}, u32[]{:S(2)}) copy-start(f32[1,1024]{1,0:T(1,128)} %get-tuple-element.191) | copy-start | bytes 12292
  598.9 399.6 %reduce-scatter.14.cloned.1.call-start = ((), (), s32[]{:S(2)}) async-start(), calls=%async_computation.21 | async-start | bytes 10485760 | tf_op jit(solution)/shard_map/reduce_scatter | solution.py:205
  618.8 79.8 %all-to-all-start.1 = ((bf16[784,4,256]{2,0,1:T(8,128)(2,1)}), bf16[784,4,256]{2,0,1:T(8,128)(2,1)S(1)}, u32[]{:S(2)}, u32[]{:S(2)}) async-start(bf16[784,4,256]{2,0,1:T(8,128)(2,1)} %bitcast.170), calls=%async_computation.1 | async-start | bytes 3211264 | tf_op jit(solution)/shard_map/all_to_all | solution.py:226
  622.3 376.9 %reduce-scatter.18.cloned.1.call-start = ((), (), s32[]{:S(2)}) async-start(), calls=%async_computation.23 | async-start | bytes 10485760 | tf_op jit(solution)/shard_map/reduce_scatter | solution.py:208
  636.6 409.9 %reduce-scatter.12.cloned.1.call-start = ((), (), s32[]{:S(2)}) async-start(), calls=%async_computation.20 | async-start | bytes 786432 | tf_op jit(solution)/shard_map/reduce_scatter | solution.py:280
  988.4 58.2 %reduce-scatter.8.cloned.1.call-start = ((), (), s32[]{:S(2)}) async-start(), calls=%async_computation.18 | async-start | bytes 2359296 | tf_op jit(solution)/shard_map/reduce_scatter | solution.py:277
  998.4 48.1 %reduce-scatter.16.cloned.1.call-start = ((), (), s32[]{:S(2)}) async-start(), calls=%async_computation.22 | async-start | bytes 3145728 | tf_op jit(solution)/shard_map/reduce_scatter | solution.py:283
  999.2 47.4 %reduce-scatter.20.cloned.1.call-start = ((), (), s32[]{:S(2)}) async-start(), calls=%async_computation.24 | async-start | bytes 3145728 | tf_op jit(solution)/shard_map/reduce_scatter | solution.py:286
  999.8 299.5 %all-gather.23.cloned.1.call-start = ((), (), s32[]{:S(2)}) async-start(), calls=%async_computation.17 | async-start | bytes 7864320 | tf_op jit(solution)/shard_map/all_gather | solution.py:177
  1037.0 244.6 %all-to-all-start.2 = ((bf16[3136,3,256]{2,1,0:T(4,128)(2,1)}), bf16[3136,3,256]{2,1,0:T(4,128)(2,1)}, u32[]{:S(2)}, u32[]{:S(2)}) async-start(bf16[3136,3,256]{2,1,0:T(4,128)(2,1)} %reshape.166), calls=%async_computation.2 | async-start | bytes 12845056 | tf_op jit(solution)/shard_map/all_to_all | solution.py:240
  1042.3 319.6 %all-reduce.4.cloned.1.call-start = ((), (), s32[]{:S(2)}) async-start(), calls=%async_computation.25 | async-start | bytes 6291456 | tf_op jit(solution)/shard_map/psum | solution.py:291
  (66 other events, 710.8 us)
Sparse Core Ops, SparseCore 0:
  9.6 13.2 all-gather.14
  24.5 11.7 all-gather.18
  38.4 10.9 all-gather.10
  51.4 118.6 all-gather.8
  171.5 44.1 all-gather.12
  217.1 182.7 all-gather.16
  401.5 147.7 all-gather.20
  599.0 55.7 reduce-scatter.9
  657.3 151.0 reduce-scatter.13
  810.7 145.4 reduce-scatter.17
  988.5 6.2 reduce-scatter.11
  998.6 9.0 reduce-scatter.7
  1010.0 10.8 reduce-scatter.15
  1023.0 10.7 reduce-scatter.19
  1035.3 229.2 all-gather.22
  1268.2 93.6 all-reduce.3
where the time goes:
time: 1380 us
  waiting for transfers between devices  577 us (42%)
  matrix products  359 us (26%)
  local copies, waits for them, and re-layouts  159 us (12%)
  blocking collectives  121 us (9%)
  other arithmetic  112 us (8%)
  loops' own time  17.3 us (1%)
  between operations  17.3 us (1%)
    all_to_all x1, waiting for transfers between devices, local(): lax.all_to_all(grads_packed.reshape(group_rows, 3, head_width), 'col', sp...  235 us
    all_gather x1, waiting for transfers between devices, local(): lax.all_gather(fc2_full, 'col', axis=0, tiled=True)  121 us
    all_gather x1, waiting for transfers between devices, local(): tokens_one = lax.all_gather(norm_one, 'col', axis=0, tiled=True)  121 us
    dot_general x8, matrix products, masked_scores(): jnp.einsum('ihd,jhd->hij', queries, key_rows, preferred_element_type=jnp....  82.4 us
    all_gather x1, blocking collectives, local(): lax.all_gather(fc1_bias, 'col', axis=0, tiled=True)  78 us
    all_to_all x1, waiting for transfers between devices, local(): lax.all_to_all(grad_attended_rows, 'col', split_axis=1, concat_axis=0, ti...  61.9 us
    convert_element_type x4, local copies, waits for them, and re-layouts, local(): grads_packed.reshape(group_rows, 3 * head_width).astype(jnp.bfloat16)  57.5 us
    convert_element_type x4, other arithmetic, attend_clip_back(): grad_logits = (probs * (grad_probs - jnp.sum(probs * grad_probs, axis=-1,...  56.2 us
  transfers between devices with their start and end apart: 19, of which 8 were waited for; matrix products, arithmetic and copies ran while one was open for 41% of the time, Pallas kernels for 0%

commit v1 on v0

--- a/solution.py
+++ b/solution.py
@@ -1,3 +1,4 @@
+import functools
 import jax
 import jax.numpy as jnp
 from jax import lax
@@ -9,6 +10,13 @@
 MASKED = -1e30
 ROOT_HALF = 0.7071067811865476
 DENSITY_FACTOR = 0.3989422804014327
+
+
+def mix_figure(x_part, a_name, along_axis):
+    return lax.psum(lax.psum(x_part, a_name), along_axis)
+
+
+mark_zones = functools.partial(mix_figure, a_name=("row", "col"), along_axis="dp")
 
 
 def normalize(values, factor, offset):
@@ -270,8 +278,8 @@
         jnp.stack([bias_sums[0], bias_sums[2]]),
         (0, col_index * head_width),
     )
-    token_sums, head_sums, fc1_sums, loss_sum = lax.psum(
-        (token_vectors, head_vectors, fc1_bias_sum, numerator), ("dp", "row", "col")
+    token_sums, head_sums, fc1_sums, loss_sum = mark_zones(
+        (token_vectors, head_vectors, fc1_bias_sum, numerator)
     )
     qkv_rows, proj_cols, fc1_rows, fc2_cols = (
         lax.psum_scatter(

time: 1380 us -> 1390 us (level)
    psum x1 -> x2, blocking collectives: 39.1 us -> 46.5 us  [mix_figure(): return lax.psum(lax.psum(x_part, a_name), along_axis)]
  transfers between devices with their start and end apart: 19 -> 19, of which waited for: 8 -> 7; matrix products, arithmetic and copies ran while one was open for 41% -> 41% of each run, Pallas kernels for 0% -> 0%
where the time goes in v1:
time: 1390 us; the launch traced here: 1380 us
  waiting for transfers between devices  571 us (41%)
  matrix products  359 us (26%)
  local copies, waits for them, and re-layouts  159 us (11%)
  blocking collectives  129 us (9%)
  other arithmetic  112 us (8%)
  loops' own time  17.3 us (1%)
  between operations  17.3 us (1%)
    all_to_all x1, waiting for transfers between devices, local(): lax.all_to_all(grads_packed.reshape(group_rows, 3, head_width), 'col', sp...  235 us
    all_gather x1, waiting for transfers between devices, local(): lax.all_gather(fc2_full, 'col', axis=0, tiled=True)  121 us
    all_gather x1, waiting for transfers between devices, local(): tokens_one = lax.all_gather(norm_one, 'col', axis=0, tiled=True)  121 us
    dot_general x8, matrix products, masked_scores(): jnp.einsum('ihd,jhd->hij', queries, key_rows, preferred_element_type=jnp....  82.5 us
    all_gather x1, blocking collectives, local(): lax.all_gather(fc1_bias, 'col', axis=0, tiled=True)  78 us
    all_to_all x1, waiting for transfers between devices, local(): lax.all_to_all(grad_attended_rows, 'col', split_axis=1, concat_axis=0, ti...  61.9 us
    convert_element_type x4, local copies, waits for them, and re-layouts, local(): grads_packed.reshape(group_rows, 3 * head_width).astype(jnp.bfloat16)  57.6 us
    convert_element_type x4, other arithmetic, attend_clip_back(): grad_logits = (probs * (grad_probs - jnp.sum(probs * grad_probs, axis=-1,...  56.2 us
  transfers between devices with their start and end apart: 19, of which 7 were waited for; matrix products, arithmetic and copies ran while one was open for 41% of the time, Pallas kernels for 0%

profile of v1, /device:TPU:0, one launch (start us, length us, event | category | flops | bytes accessed | tf_op | source)
XLA Modules:
  0.0 1378.2 jit_solution(15634704702560019353)
XLA Ops:
  49.4 120.7 %all-gather.9.cloned.1.call-done = bf16[3136,1024]{1,0:T(8,128)(2,1)} async-done(((bf16[784,1024]{1,0:T(8,128)(2,1)}), bf16[3136,1024]{1,0:T(8,128)(2,1)}) %all-gather.9.cloned.1.call-update) | async-done | bytes 6422544 | tf_op jit(solution)/shard_map/all_gather | solution.py:165
  179.4 14.6 %reshape.167 = bf16[2,1568,3,4,64]{4,3,1,0,2:T(4,128)(2,1)} reshape(bf16[3136,3,256]{2,0,1:T(8,128)(2,1)} %add_convert_fusion) | data formatting | bytes 9633792 | tf_op jit(solution)/shard_map/reshape | solution.py:178
  194.0 15.6 %copy.62 = bf16[2,1568,3,4,64]{1,4,3,2,0:T(8,128)(2,1)} copy(bf16[2,1568,3,4,64]{4,3,1,0,2:T(4,128)(2,1)} %reshape.167) | data formatting | bytes 9633792 | tf_op jit(solution)/shard_map/while | solution.py:179
  209.6 100.1 %while.22 = (s32[]{:T(128)}, bf16[2,1568,4,64]{1,3,2,0:T(8,128)(2,1)S(1)}, f32[2,4,1568]{2,1,0:T(4,128)S(1)}, bf16[2,1568,3,4,64]{1,4,3,2,0:T(8,128)(2,1)}, s32[2]{0:T(128)S(1)}, /*index=5*/s32[]{:T(128)}) while((s32[]{:T(128)}, bf16[2,1568,4,64]{1,3,2,0:T(8,128)(2,1)S(1)}, f32[2,4,1568]{2,1,0:T(4,128)S(1)}, ...), condition=%wide.region_7.8_spmd, body=%wide.region_2.7_spmd.sunk | while | flops 2588079616 | bytes 208644768 | solution.py:179
  324.4 78.0 %all_gather.40 = bf16[4096]{0:T(1024)(128)(2,1)S(1)} all-gather(bf16[1024]{0:T(1024)(128)(2,1)S(1)} %copy-done.38), channel_id=1, replica_groups=mesh['dp'=4,'row'=2,'col'=4] {'col'}, dimensions={0}, use_global_device_ids=true | all-gather | bytes 10240 | tf_op jit(solution)/shard_map/all_gather | solution.py:196
  412.2 15.9 %multiply_convert_fusion.2 = (bf16[784,4096]{1,0:T(8,128)(2,1)}, f32[784,4096]{1,0:T(8,128)}) fusion(f32[4096]{0:T(1024)S(1)} %convert_element_type.142, bf16[1024,4096]{1,0:T(8,128)(2,1)} %all-gather.17.cloned.1.call-done, f32[784,1024]{1,0:T(8,128)} %copy-done.10, f32[1024]{0:T(1024)S(1)} %bitcast.272, f32[1024]{0:T(1024)S(1)} %bitcast.262, ...), kind=kOutput, calls=%fused_computation.70 | convolution fusion | flops 6599950336 | bytes 30898304 | tf_op jit(solution)/shard_map/dot_general | solution.py:198
  428.0 121.3 %all-gather.21.cloned.1.call-done = bf16[4096,1024]{1,0:T(8,128)(2,1)} async-done(((bf16[1024,1024]{1,0:T(8,128)(2,1)}), bf16[4096,1024]{1,0:T(8,128)(2,1)}) %all-gather.21.cloned.1.call-update) | async-done | bytes 8388624 | tf_op jit(solution)/shard_map/all_gather | solution.py:195
  561.7 17.8 %convert_reduce_fusion = (f32[4096]{0:T(1024)}, bf16[784,4096]{1,0:T(8,128)(2,1)}) fusion(f32[784,4096]{1,0:T(8,128)} %get-tuple-element.206, f32[4096]{0:T(1024)S(1)} %convert_element_type.142, bf16[784,1024]{1,0:T(8,128)(2,1)S(1)} %get-tuple-element.166, bf16[4096,1024]{1,0:T(8,128)(2,1)} %all-gather.21.cloned.1.call-done), kind=kOutput, calls=%fused_computation.69 | convolution fusion | flops 6618411008 | bytes 29294592 | tf_op jit(solution)/shard_map/dot_general | solution.py:208
  598.9 15.1 %convolution_convert_fusion = bf16[1024,4096]{1,0:T(8,128)(2,1)} fusion(bf16[784,4096]{1,0:T(8,128)(2,1)} %get-tuple-element.211, f32[784,1024]{1,0:T(8,128)} %copy-done.10, f32[1024]{0:T(1024)S(1)} %bitcast.273, f32[1024]{0:T(1024)S(1)} %bitcast.265, f32[784]{0:T(1024)S(1)} %add_rsqrt_fusion, f32[784]{0:T(1024)S(1)} %broadcast_multiply_fusion.5), kind=kOutput, calls=%fused_computation.74 | convolution fusion | flops 6584877056 | bytes 18036864 | tf_op jit(solution)/shard_map/dot_general | solution.py:211
  622.4 14.2 %convolution_convert_fusion.1 = bf16[4096,1024]{1,0:T(8,128)(2,1)} fusion(bf16[784,4096]{1,0:T(8,128)(2,1)} %get-tuple-element.205, bf16[784,1024]{1,0:T(8,128)(2,1)S(1)} %copy-done.52), kind=kOutput, calls=%fused_computation.75 | convolution fusion | flops 6580862976 | bytes 16416768 | tf_op jit(solution)/shard_map/dot_general | solution.py:210
  636.7 61.9 %all-to-all-done.1 = bf16[784,4,256]{2,0,1:T(8,128)(2,1)S(1)} async-done(((bf16[784,4,256]{2,0,1:T(8,128)(2,1)}), bf16[784,4,256]{2,0,1:T(8,128)(2,1)S(1)}, u32[]{:S(2)}, u32[]{:S(2)}) %all-to-all-start.1) | async-done | bytes 1605664 | tf_op jit(solution)/shard_map/all_to_all | solution.py:234
  709.0 258.5 %while.23 = (s32[]{:T(128)}, bf16[2,1568,3,4,64]{1,4,3,2,0:T(8,128)(2,1)}, bf16[2,1568,3,4,64]{1,4,3,2,0:T(8,128)(2,1)}, s32[2]{0:T(128)S(1)}, f32[2,4,1568]{2,1...) while((s32[]{:T(128)}, bf16[2,1568,3,4,64]{1,4,3,2,0:T(8,128)(2,1)}, ...), condition=%wide.region_19.20_spmd, body=%wide.region_16.19_spmd.sunk | while | flops 6394224128 | bytes 484584864 | solution.py:237
  740.5 14.7 %multiply_reduce_fusion.9 = (f32[4,784]{1,0:T(4,128)S(1)}, f32[4,784,1568]{2,1,0:T(8,128)}) fusion(f32[4,784,1568]{2,1,0:T(8,128)} %fusion.126, f32[4,784]{1,0:T(4,128)S(1)} %get-tuple-element.300, bf16[1568,3,4,64]{0,3,2,1:T(8,128)(2,1)S(1)} %dynamic-slice_bitcast_fusion.21, pred[1568]{0:T(1024)(128)(4,1)S(1)} %iota_compare_fusion.6), kind=kOutput, calls=%fused_computation.25.clone.1 | convolution fusion | flops 653990848 | bytes 40677632 | tf_op jit(solution)/shard_map/while/body/eval_jaxpr/ihd,jhd->hij/dot_general | solution.py:48
  783.9 14.1 %multiply_reduce_fusion.10 = (f32[4,784]{1,0:T(4,128)S(1)}, f32[4,784,1568]{2,1,0:T(8,128)}) fusion(f32[4,784,1568]{2,1,0:T(8,128)} %fusion.129, f32[4,784]{1,0:T(4,128)S(1)} %get-tuple-element.302, bf16[1568,3,4,64]{0,3,2,1:T(8,128)(2,1)S(1)} %dynamic-slice_bitcast_fusion.21, pred[1568]{0:T(1024)(128)(4,1)S(1)} %iota_compare_fusion.6), kind=kOutput, calls=%fused_computation.28.clone.1 | convolution fusion | flops 653990848 | bytes 40677632 | tf_op jit(solution)/shard_map/while/body/eval_jaxpr/ihd,jhd->hij/dot_general | solution.py:48
  798.0 13.9 %multiply_convert_fusion.7 = bf16[4,784,1568]{2,1,0:T(8,128)(2,1)S(1)} fusion(f32[4,784,1568]{2,1,0:T(8,128)} %get-tuple-element.303, f32[4,784,1568]{2,1,0:T(8,128)} %fusion.129, f32[4,784]{1,0:T(4,128)S(1)} %get-tuple-element.304), kind=kLoop, calls=%fused_computation.27.clone.1 | loop fusion | flops 14751744 | bytes 49185024 | tf_op jit(solution)/shard_map/while/body/eval_jaxpr/convert_element_type | solution.py:95
  861.6 14.6 %multiply_reduce_fusion.9 = (f32[4,784]{1,0:T(4,128)S(1)}, f32[4,784,1568]{2,1,0:T(8,128)}) fusion(f32[4,784,1568]{2,1,0:T(8,128)} %fusion.126, f32[4,784]{1,0:T(4,128)S(1)} %get-tuple-element.300, bf16[1568,3,4,64]{0,3,2,1:T(8,128)(2,1)S(1)} %dynamic-slice_bitcast_fusion.21, pred[1568]{0:T(1024)(128)(4,1)S(1)} %iota_compare_fusion.6), kind=kOutput, calls=%fused_computation.25.clone.1 | convolution fusion | flops 653990848 | bytes 40677632 | tf_op jit(solution)/shard_map/while/body/eval_jaxpr/ihd,jhd->hij/dot_general | solution.py:48
  876.1 14.5 %multiply_convert_fusion.8 = bf16[4,784,1568]{2,1,0:T(8,128)(2,1)S(1)} fusion(f32[4,784,1568]{2,1,0:T(8,128)} %get-tuple-element.301, f32[4,784,1568]{2,1,0:T(8,128)} %fusion.126, f32[4,784]{1,0:T(4,128)S(1)} %get-tuple-element.305), kind=kLoop, calls=%fused_computation.24.clone.1 | loop fusion | flops 14751744 | bytes 49185024 | tf_op jit(solution)/shard_map/while/body/eval_jaxpr/convert_element_type | solution.py:95
  905.6 14.0 %multiply_reduce_fusion.10 = (f32[4,784]{1,0:T(4,128)S(1)}, f32[4,784,1568]{2,1,0:T(8,128)}) fusion(f32[4,784,1568]{2,1,0:T(8,128)} %fusion.129, f32[4,784]{1,0:T(4,128)S(1)} %get-tuple-element.302, bf16[1568,3,4,64]{0,3,2,1:T(8,128)(2,1)S(1)} %dynamic-slice_bitcast_fusion.21, pred[1568]{0:T(1024)(128)(4,1)S(1)} %iota_compare_fusion.6), kind=kOutput, calls=%fused_computation.28.clone.1 | convolution fusion | flops 653990848 | bytes 40677632 | tf_op jit(solution)/shard_map/while/body/eval_jaxpr/ihd,jhd->hij/dot_general | solution.py:48
  919.5 13.9 %multiply_convert_fusion.7 = bf16[4,784,1568]{2,1,0:T(8,128)(2,1)S(1)} fusion(f32[4,784,1568]{2,1,0:T(8,128)} %get-tuple-element.303, f32[4,784,1568]{2,1,0:T(8,128)} %fusion.129, f32[4,784]{1,0:T(4,128)S(1)} %get-tuple-element.304), kind=kLoop, calls=%fused_computation.27.clone.1 | loop fusion | flops 14751744 | bytes 49185024 | tf_op jit(solution)/shard_map/while/body/eval_jaxpr/convert_element_type | solution.py:95
  1000.4 16.1 %copy.80 = bf16[2,1568,3,4,64]{4,3,2,1,0:T(4,128)(2,1)} copy(bf16[2,1568,3,4,64]{1,4,3,2,0:T(8,128)(2,1)} %get-tuple-element.78) | data formatting | bytes 9633792 | tf_op jit(solution)/shard_map/convert_element_type | solution.py:243
  1016.5 20.6 %reshape.166 = bf16[3136,3,256]{2,1,0:T(4,128)(2,1)} reshape(bf16[2,1568,3,4,64]{4,3,2,1,0:T(4,128)(2,1)} %copy.80) | data formatting | bytes 9633792 | tf_op jit(solution)/shard_map/convert_element_type | solution.py:243
  1046.7 234.9 %all-to-all-done.2 = bf16[3136,3,256]{2,1,0:T(4,128)(2,1)} async-done(((bf16[3136,3,256]{2,1,0:T(4,128)(2,1)}), bf16[3136,3,256]{2,1,0:T(4,128)(2,1)}, u32[]{:S(2)}, u32[]{:S(2)}) %all-to-all-start.2) | async-done | bytes 4816928 | tf_op jit(solution)/shard_map/all_to_all | solution.py:248
  1310.1 26.9 %all-reduce = (f32[]{:T(128)}, f32[6,1024]{1,0:T(8,128)S(1)}, f32[2,1024]{1,0:T(2,128)S(1)}, f32[4096]{0:T(1024)S(1)}) all-reduce(f32[]{:T(128)} %get-tuple-element.185, f32[6,1024]{1,0:T(8,128)S(1)} %stack.90, f32[2,1024]{1,0:T(2,128)S(1)} %maximum_dynamic-update-slice_fusion, ...), channel_id=1, replica_groups=mesh['dp'=4,'row'=2,'col'=4] {'row','col'}, use_global_device_ids=true, to_apply=%region_11.12 | all-reduce | flops 12289 | bytes 98312 | tf_op jit(solution)/shard_map/psum | solution.py:16
  1337.0 19.6 %all-reduce.1 = (f32[]{:T(128)}, f32[6,1024]{1,0:T(8,128)S(1)}, f32[2,1024]{1,0:T(2,128)S(1)}, f32[4096]{0:T(1024)S(1)}) all-reduce(f32[]{:T(128)} %get-tuple-element.153, f32[6,1024]{1,0:T(8,128)S(1)} %get-tuple-element.154, f32[2,1024]{1,0:T(2,128)S(1)} %get-tuple-element.155, ...), channel_id=1, replica_groups=mesh['dp'=4,'row'=2,'col'=4] {'dp'}, use_global_device_ids=true, to_apply=%region_12.13 | all-reduce | flops 12289 | bytes 98312 | tf_op jit(solution)/shard_map/psum | solution.py:16
  (320 shorter events, 450.7 us)
Async XLA Ops:
  7.3 15.7 %all-gather.15.cloned.1.call-start = ((), (), s32[]{:S(2)}) async-start(), calls=%async_computation.13 | async-start | bytes 3145728 | tf_op jit(solution)/shard_map/all_gather | solution.py:143
  8.0 28.3 %all-gather.19.cloned.1.call-start = ((), (), s32[]{:S(2)}) async-start(), calls=%async_computation.15 | async-start | bytes 3145728 | tf_op jit(solution)/shard_map/all_gather | solution.py:144
  8.7 40.7 %all-gather.11.cloned.1.call-start = ((), (), s32[]{:S(2)}) async-start(), calls=%async_computation.11 | async-start | bytes 2359296 | tf_op jit(solution)/shard_map/all_gather | solution.py:141
  11.1 159.0 %all-gather.9.cloned.1.call-start = ((), (), s32[]{:S(2)}) async-start(), calls=%async_computation.10 | async-start | bytes 8028160 | tf_op jit(solution)/shard_map/all_gather | solution.py:165
  17.2 388.2 %all-gather.13.cloned.1.call-start = ((), (), s32[]{:S(2)}) async-start(), calls=%async_computation.12 | async-start | bytes 2621440 | tf_op jit(solution)/shard_map/all_gather | solution.py:184
  19.6 392.5 %all-gather.17.cloned.1.call-start = ((), (), s32[]{:S(2)}) async-start(), calls=%async_computation.14 | async-start | bytes 10485760 | tf_op jit(solution)/shard_map/all_gather | solution.py:194
  23.0 526.3 %all-gather.21.cloned.1.call-start = ((), (), s32[]{:S(2)}) async-start(), calls=%async_computation.16 | async-start | bytes 10485760 | tf_op jit(solution)/shard_map/all_gather | solution.py:195
  317.6 84.9 %copy-start.46 = (s32[16]{0:T(128)S(1)}, s32[16]{0:T(128)}, u32[]{:S(2)}) copy-start(s32[16]{0:T(128)} %param.37) | copy-start | bytes 196
  317.6 85.1 %copy-start.22 = (s32[25088]{0:T(1024)S(1)}, s32[25088]{0:T(1024)}, u32[]{:S(2)}) copy-start(s32[25088]{0:T(1024)} %param.36) | copy-start | bytes 301060
  320.6 84.8 %copy-start.37 = (f32[1,1024]{1,0:T(1,128)S(1)}, f32[1,1024]{1,0:T(1,128)}, u32[]{:S(2)}) copy-start(f32[1,1024]{1,0:T(1,128)} %get-tuple-element.196) | copy-start | bytes 12292
  320.6 83.4 %all-to-all-start = ((bf16[4,784,256]{2,1,0:T(8,128)(2,1)}), bf16[4,784,256]{2,1,0:T(8,128)(2,1)S(1)}, u32[]{:S(2)}, u32[]{:S(2)}) async-start(bf16[4,784,256]{2,1,0:T(8,128)(2,1)} %reshape.164), calls=%async_computation | async-start | bytes 3211264 | tf_op jit(solution)/shard_map/all_to_all | solution.py:187
  324.3 664.1 %reduce-scatter.10.cloned.1.call-start = ((), (), s32[]{:S(2)}) async-start(), calls=%async_computation.19 | async-start | bytes 2621440 | tf_op jit(solution)/shard_map/reduce_scatter | solution.py:228
  412.1 137.2 %copy-start.11 = (f32[784,1024]{1,0:T(8,128)S(1)}, f32[784,1024]{1,0:T(8,128)}, u32[]{:S(2)}) copy-start(f32[784,1024]{1,0:T(8,128)} %copy-done.10) | copy-start | bytes 9633796
  412.2 137.2 %copy-start.36 = (f32[1,1024]{1,0:T(1,128)S(1)}, f32[1,1024]{1,0:T(1,128)}, u32[]{:S(2)}) copy-start(f32[1,1024]{1,0:T(1,128)} %get-tuple-element.195) | copy-start | bytes 12292
  598.9 399.7 %reduce-scatter.14.cloned.1.call-start = ((), (), s32[]{:S(2)}) async-start(), calls=%async_computation.21 | async-start | bytes 10485760 | tf_op jit(solution)/shard_map/reduce_scatter | solution.py:213
  618.7 79.8 %all-to-all-start.1 = ((bf16[784,4,256]{2,0,1:T(8,128)(2,1)}), bf16[784,4,256]{2,0,1:T(8,128)(2,1)S(1)}, u32[]{:S(2)}, u32[]{:S(2)}) async-start(bf16[784,4,256]{2,0,1:T(8,128)(2,1)} %bitcast.170), calls=%async_computation.1 | async-start | bytes 3211264 | tf_op jit(solution)/shard_map/all_to_all | solution.py:234
  622.3 377.0 %reduce-scatter.18.cloned.1.call-start = ((), (), s32[]{:S(2)}) async-start(), calls=%async_computation.23 | async-start | bytes 10485760 | tf_op jit(solution)/shard_map/reduce_scatter | solution.py:216
  636.6 410.0 %reduce-scatter.12.cloned.1.call-start = ((), (), s32[]{:S(2)}) async-start(), calls=%async_computation.20 | async-start | bytes 786432 | tf_op jit(solution)/shard_map/reduce_scatter | solution.py:288
  988.4 58.2 %reduce-scatter.8.cloned.1.call-start = ((), (), s32[]{:S(2)}) async-start(), calls=%async_computation.18 | async-start | bytes 2359296 | tf_op jit(solution)/shard_map/reduce_scatter | solution.py:285
  998.5 48.2 %reduce-scatter.16.cloned.1.call-start = ((), (), s32[]{:S(2)}) async-start(), calls=%async_computation.22 | async-start | bytes 3145728 | tf_op jit(solution)/shard_map/reduce_scatter | solution.py:291
  999.3 47.4 %reduce-scatter.20.cloned.1.call-start = ((), (), s32[]{:S(2)}) async-start(), calls=%async_computation.24 | async-start | bytes 3145728 | tf_op jit(solution)/shard_map/reduce_scatter | solution.py:294
  999.8 299.6 %all-gather.23.cloned.1.call-start = ((), (), s32[]{:S(2)}) async-start(), calls=%async_computation.17 | async-start | bytes 7864320 | tf_op jit(solution)/shard_map/all_gather | solution.py:185
  1037.1 244.6 %all-to-all-start.2 = ((bf16[3136,3,256]{2,1,0:T(4,128)(2,1)}), bf16[3136,3,256]{2,1,0:T(4,128)(2,1)}, u32[]{:S(2)}, u32[]{:S(2)}) async-start(bf16[3136,3,256]{2,1,0:T(4,128)(2,1)} %reshape.166), calls=%async_computation.2 | async-start | bytes 12845056 | tf_op jit(solution)/shard_map/all_to_all | solution.py:248
  1042.4 321.2 %all-reduce.5.cloned.1.call-start = ((), (), s32[]{:S(2)}) async-start(), calls=%async_computation.25 | async-start | bytes 6291456 | tf_op jit(solution)/shard_map/psum | solution.py:299
  (66 other events, 710.7 us)
Sparse Core Ops, SparseCore 0:
  9.6 13.2 all-gather.14
  24.5 11.7 all-gather.18
  38.4 10.9 all-gather.10
  51.4 118.6 all-gather.8
  171.5 44.1 all-gather.12
  217.1 182.7 all-gather.16
  401.5 147.7 all-gather.20
  599.0 55.8 reduce-scatter.9
  657.3 151.0 reduce-scatter.13
  810.7 145.4 reduce-scatter.17
  988.6 6.2 reduce-scatter.11
  998.6 9.1 reduce-scatter.7
  1010.1 10.8 reduce-scatter.15
  1023.0 10.7 reduce-scatter.19
  1035.4 229.2 all-gather.22
  1268.3 94.5 all-reduce.4
